TPU v7x, 32 devices: a whole 2x2x4 slice. The times are simulated.
32 devices in a mesh: shard: 2 (over x), ctx: 4 (over z), tp: 4 (over y, core).
Axes of the slice: x: 2, y: 2, z: 4, core: 2. Of those that a mesh axis runs over, the one named last changes fastest.
Arguments:
- tokens: bfloat16 [6, 1024, 1152], P('shard', 'ctx'), may hold values from -6 to 6
- condition: bfloat16 [6, 1152], P('shard'), may hold values from -6 to 6
- ada_weight: bfloat16 [1152, 6912], P('shard'), may hold values from -0.1875 to 0.1875
- ada_bias: float32 [6912], replicated, may hold values from -3 to 3
- qkv_weight: bfloat16 [1152, 16, 216], P('shard', 'tp'), may hold values from -0.1875 to 0.1875
- qv_bias: float32 [16, 144], P('tp'), may hold values from -2 to 2
- out_weight: bfloat16 [1152, 1152], P('tp', 'shard'), may hold values from -1 to 1
- out_bias: float32 [1152], replicated, may hold values from -2 to 2
- up_weight: bfloat16 [1152, 4608], P('shard', 'tp'), may hold values from -0.1875 to 0.1875
- up_bias: float32 [4608], P('tp'), may hold values from -3 to 3
- down_weight: bfloat16 [4608, 1152], P('tp', 'shard'), may hold values from -0.09375 to 0.09375
- down_bias: float32 [1152], replicated, may hold values from -2 to 2
- cotangent: bfloat16 [6, 1024, 1152], P('shard', 'ctx'), may hold values from -6 to 6
Outputs:
- result: bfloat16 [6, 1024, 1152], P('shard', 'ctx')
- grad_tokens: float32 [6, 1024, 1152], P('shard', 'ctx')
- grad_condition: float32 [6, 1152], P('shard')
- grad_ada_weight: float32 [1152, 6912], P('shard')
- grad_ada_bias: float32 [6912], P('shard')
- grad_qkv_weight: float32 [1152, 16, 216], P('shard', 'tp')
- grad_qv_bias: float32 [16, 144], P('tp', 'shard')
- grad_out_weight: float32 [1152, 1152], P('tp', 'shard')
- grad_out_bias: float32 [1152], P('shard')
- grad_up_weight: float32 [1152, 4608], P('shard', 'tp')
- grad_up_bias: float32 [4608], P(('tp', 'shard'))
- grad_down_weight: float32 [4608, 1152], P('tp', 'shard')
- grad_down_bias: float32 [1152], P('shard')
All inputs are finite; a program needn't handle non-finite values.
Results may differ from a plain program's by a relative error of at most 0.02.
The roundings to bfloat16 on the way count: a program that leaves them out, or rounds other values in their place, can miss the bound.
Values may be sent and summed in bfloat16 or wider, within the bound.
A program may use at most 192 MiB of HBM per device.

v0:
```python
import jax
import jax.numpy as jnp
from jax import lax
from jax.sharding import PartitionSpec as P


def layer_norm(values):
    row_mean = jnp.mean(values, -1, keepdims=True)
    centered = values - row_mean
    variance = jnp.mean(centered * centered, -1, keepdims=True)
    return centered * lax.rsqrt(variance + 1e-06)


def modulate(values, shift_row, scale_row):
    return layer_norm(values) * (1.0 + scale_row[:, None, :]) + shift_row[:, None, :]


def gelu_tanh(values):
    return (
        0.5
        * values
        * (1.0 + jnp.tanh(0.7978845608028654 * (values + 0.044715 * values * values * values)))
    )


def silu_act(values):
    return values * jax.nn.sigmoid(values)


def contract_rows(left, right):
    return lax.dot_general(
        left, right, (((0,), (0,)), ((), ())), preferred_element_type=jnp.float32
    )


def contract_cols(left, right):
    return lax.dot_general(
        left, right, (((1,), (1,)), ((), ())), preferred_element_type=jnp.float32
    )


def attend_forward(packed):
    head_size = packed.shape[-1] // 3

    def one_latent(latent_qkv):
        query_part = latent_qkv[..., :head_size]
        key_part = latent_qkv[..., head_size : 2 * head_size]
        value_part = latent_qkv[..., 2 * head_size :]
        scores = jnp.einsum(
            "shd,thd->hst", query_part, key_part, preferred_element_type=jnp.float32
        ) * head_size ** (-0.5)
        row_max = jnp.max(scores, -1, keepdims=True)
        exponent = jnp.exp(scores - row_max)
        exp_total = jnp.sum(exponent, -1, keepdims=True)
        probability = (exponent / exp_total).astype(jnp.bfloat16)
        attended = jnp.einsum(
            "hst,thd->shd", probability, value_part, preferred_element_type=jnp.float32
        )
        log_total = (row_max + jnp.log(exp_total))[..., 0]
        return (attended.astype(jnp.bfloat16), log_total)

    attended, log_total = lax.map(one_latent, packed)
    return (attended, log_total, packed)


def attend_backward(inputs):
    latent_qkv, log_total, grad_out = inputs
    head_size = latent_qkv.shape[-1] // 3
    scale_factor = head_size ** (-0.5)
    query_part = latent_qkv[..., :head_size]
    key_part = latent_qkv[..., head_size : 2 * head_size]
    value_part = latent_qkv[..., 2 * head_size :]
    scores = (
        jnp.einsum("shd,thd->hst", query_part, key_part, preferred_element_type=jnp.float32)
        * scale_factor
    )
    probability = jnp.exp(scores - log_total[..., None])
    prob_low = probability.astype(jnp.bfloat16)
    grad_prob = jnp.einsum("shd,thd->hst", grad_out, value_part, preferred_element_type=jnp.float32)
    row_dot = jnp.sum(probability * grad_prob, -1, keepdims=True)
    grad_scores = (probability * (grad_prob - row_dot)).astype(jnp.bfloat16)
    grad_query = (
        jnp.einsum("hst,thd->shd", grad_scores, key_part, preferred_element_type=jnp.float32)
        * scale_factor
    )
    grad_key = (
        jnp.einsum("hst,shd->thd", grad_scores, query_part, preferred_element_type=jnp.float32)
        * scale_factor
    )
    grad_value = jnp.einsum("hst,shd->thd", prob_low, grad_out, preferred_element_type=jnp.float32)
    return jnp.concatenate([grad_query, grad_key, grad_value], -1).astype(jnp.bfloat16)


def swap(values, axis, distance):
    count = lax.axis_size(axis)
    return lax.ppermute(values, axis, [(i, i ^ distance) for i in range(count)])


def gather_shard(values, axis):
    if lax.axis_size("shard") != 2:
        return lax.all_gather(values, "shard", axis=axis, tiled=True)
    other = swap(values, "shard", 1)
    first = lax.axis_index("shard") == 0
    return jnp.concatenate([jnp.where(first, values, other), jnp.where(first, other, values)], axis)


def scatter_shard(values, axis):
    count = lax.axis_size("shard")
    if count != 2:
        return lax.psum_scatter(
            values.astype(jnp.bfloat16), "shard", scatter_dimension=axis, tiled=True
        ).astype(jnp.float32)
    half = values.shape[axis] // 2
    low = lax.slice_in_dim(values, 0, half, axis=axis)
    high = lax.slice_in_dim(values, half, 2 * half, axis=axis)
    first = lax.axis_index("shard") == 0
    sent = jnp.where(first, high, low).astype(jnp.bfloat16)
    kept = jnp.where(first, low, high)
    return kept + swap(sent, "shard", 1).astype(jnp.float32)


def sum_axis(values, axis):
    count = lax.axis_size(axis)
    if count & count - 1:
        return lax.psum(values, axis)
    distance = 1
    while distance < count:
        values = values + swap(values, axis, distance)
        distance *= 2
    return values


def local(
    tokens,
    condition,
    ada_weight,
    ada_bias,
    qkv_weight,
    qv_bias,
    out_weight,
    out_bias,
    up_weight,
    up_bias,
    down_weight,
    down_bias,
    cotangent,
):
    lat_count, local_len, model_width = tokens.shape
    head_local = qkv_weight.shape[1]
    head_size = qv_bias.shape[1] // 2
    row_count = lat_count * local_len
    shard_count = lax.axis_size("shard")
    shard_at = lax.axis_index("shard")
    stored = ada_weight.shape[0]
    cond_float = condition.astype(jnp.float32)
    cond_act = silu_act(cond_float).astype(jnp.bfloat16)
    cond_all = (
        lax.all_gather(cond_act, "shard", axis=0, tiled=True)
        if shard_count != 2
        else gather_shard(cond_act, 0)
    )
    cond_mine = lax.dynamic_slice_in_dim(cond_all, shard_at * stored, stored, 1)
    mod_part = jnp.dot(cond_mine, ada_weight, preferred_element_type=jnp.float32)
    if shard_count == 2:
        first = shard_at == 0
        mod_low, mod_high = (mod_part[:lat_count], mod_part[lat_count:])
        mod_raw = jnp.where(first, mod_low, mod_high) + swap(
            jnp.where(first, mod_high, mod_low), "shard", 1
        )
    else:
        mod_raw = lax.psum_scatter(mod_part, "shard", scatter_dimension=0, tiled=True)
    qkv_full = gather_shard(qkv_weight.reshape(stored, -1), 0)
    out_full = gather_shard(out_weight, 1)
    up_full = gather_shard(up_weight, 0)
    down_full = gather_shard(down_weight, 1)
    modulation = (mod_raw + ada_bias).reshape(lat_count, 6, model_width)
    tok_float = tokens.astype(jnp.float32)
    normed = (
        modulate(tok_float, modulation[:, 0], modulation[:, 1])
        .astype(jnp.bfloat16)
        .reshape(row_count, model_width)
    )
    qkv_bias = jnp.concatenate(
        [
            qv_bias[:, :head_size],
            jnp.zeros((head_local, head_size), jnp.float32),
            qv_bias[:, head_size:],
        ],
        1,
    )
    qkv_flat = qkv_full
    packed = jnp.dot(normed, qkv_flat, preferred_element_type=jnp.float32).reshape(
        lat_count, local_len, head_local, 3 * head_size
    )
    packed = (packed + qkv_bias).astype(jnp.bfloat16)
    attended, log_total, head_packed = attend_forward(
        lax.all_to_all(packed, "ctx", split_axis=2, concat_axis=1, tiled=True)
    )
    attn_rows = lax.all_to_all(attended, "ctx", split_axis=1, concat_axis=2, tiled=True).reshape(
        row_count, head_local * head_size
    )
    branch = (
        lax.psum(
            jnp.dot(attn_rows, out_full, preferred_element_type=jnp.float32).astype(jnp.bfloat16),
            "tp",
        ).astype(jnp.float32)
        + out_bias
    )
    branch = branch.reshape(lat_count, local_len, model_width)
    middle = tok_float + modulation[:, 2][:, None, :] * branch
    normed_two = (
        modulate(middle, modulation[:, 3], modulation[:, 4])
        .astype(jnp.bfloat16)
        .reshape(row_count, model_width)
    )
    up_proj = jnp.dot(normed_two, up_full, preferred_element_type=jnp.float32) + up_bias
    activated = gelu_tanh(up_proj).astype(jnp.bfloat16)
    down_proj = (
        lax.psum(
            jnp.dot(activated, down_full, preferred_element_type=jnp.float32).astype(jnp.bfloat16),
            "tp",
        ).astype(jnp.float32)
        + down_bias
    )
    down_proj = down_proj.reshape(lat_count, local_len, model_width)
    result = (middle + modulation[:, 5][:, None, :] * down_proj).astype(jnp.bfloat16)
    grad_out = cotangent.astype(jnp.float32)
    grad_gate2 = jnp.sum(grad_out * down_proj, 1)
    grad_down = grad_out * modulation[:, 5][:, None, :]
    grad_down_bias = jnp.sum(grad_down, (0, 1))
    grad_down_low = grad_down.astype(jnp.bfloat16).reshape(row_count, model_width)
    grad_act = contract_cols(grad_down_low, down_full)
    grad_down_weight = contract_rows(activated, grad_down_low)
    grad_up = jax.vjp(gelu_tanh, up_proj)[1](grad_act)[0]
    grad_up_bias = jnp.sum(grad_up, 0)
    grad_up_low = grad_up.astype(jnp.bfloat16)
    grad_up_weight = contract_rows(normed_two, grad_up_low)
    grad_normed_two = (
        lax.psum(contract_cols(grad_up_low, up_full).astype(jnp.bfloat16), "tp")
        .astype(jnp.float32)
        .reshape(lat_count, local_len, model_width)
    )
    pull_two = jax.vjp(modulate, middle, modulation[:, 3], modulation[:, 4])[1]
    grad_middle_norm, grad_shift2, grad_scale2 = pull_two(grad_normed_two)
    grad_middle = grad_out + grad_middle_norm
    grad_gate1 = jnp.sum(grad_middle * branch, 1)
    grad_branch = grad_middle * modulation[:, 2][:, None, :]
    grad_out_bias = jnp.sum(grad_branch, (0, 1))
    grad_branch_low = grad_branch.astype(jnp.bfloat16).reshape(row_count, model_width)
    grad_out_weight = contract_rows(attn_rows, grad_branch_low)
    grad_attended = (
        contract_cols(grad_branch_low, out_full)
        .astype(jnp.bfloat16)
        .reshape(lat_count, local_len, head_local, head_size)
    )
    grad_heads = lax.all_to_all(grad_attended, "ctx", split_axis=2, concat_axis=1, tiled=True)
    grad_packed_heads = lax.map(attend_backward, (head_packed, log_total, grad_heads))
    grad_packed = lax.all_to_all(grad_packed_heads, "ctx", split_axis=1, concat_axis=2, tiled=True)
    bias_sums = jnp.sum(grad_packed.astype(jnp.float32), (0, 1))
    grad_qv_bias = jnp.concatenate([bias_sums[:, :head_size], bias_sums[:, 2 * head_size :]], 1)
    grad_packed_rows = grad_packed.reshape(row_count, head_local * 3 * head_size)
    grad_qkv_weight = contract_rows(normed, grad_packed_rows)
    grad_normed = (
        lax.psum(contract_cols(grad_packed_rows, qkv_flat).astype(jnp.bfloat16), "tp")
        .astype(jnp.float32)
        .reshape(lat_count, local_len, model_width)
    )
    pull_one = jax.vjp(modulate, tok_float, modulation[:, 0], modulation[:, 1])[1]
    grad_tokens_norm, grad_shift1, grad_scale1 = pull_one(grad_normed)
    grad_tokens = grad_middle + grad_tokens_norm
    grad_mod_part = jnp.stack(
        [grad_shift1, grad_scale1, grad_gate1, grad_shift2, grad_scale2, grad_gate2], 1
    )
    small = jnp.concatenate(
        [
            grad_mod_part.reshape(-1),
            grad_qv_bias.reshape(-1),
            grad_out_bias,
            grad_up_bias,
            grad_down_bias,
        ]
    )
    small = sum_axis(small, "ctx")
    mod_count = lat_count * 6 * model_width
    grad_modulation = small[:mod_count].reshape(lat_count, 6 * model_width)
    bias_part = small[mod_count:]
    if shard_count == 2:
        other = swap(small, "shard", 1)
        other_mod = other[:mod_count].reshape(lat_count, 6 * model_width)
        grad_mod_all = jnp.concatenate(
            [
                jnp.where(first, grad_modulation, other_mod),
                jnp.where(first, other_mod, grad_modulation),
            ],
            0,
        )
        bias_all = bias_part + other[mod_count:]
    else:
        grad_mod_all = lax.all_gather(grad_modulation, "shard", axis=0, tiled=True)
        bias_all = lax.psum(bias_part, "shard")
    grad_ada_bias_all = jnp.sum(grad_mod_all, 0)
    grad_ada_bias = lax.dynamic_slice_in_dim(
        grad_ada_bias_all,
        shard_at * (6 * model_width // shard_count),
        6 * model_width // shard_count,
        0,
    )
    grad_mod_low = grad_mod_all.astype(jnp.bfloat16)
    grad_ada_weight = contract_rows(cond_mine, grad_mod_low)
    grad_cond_part = contract_cols(grad_mod_low, ada_weight)
    if shard_count == 2:
        part_low, part_high = (grad_cond_part[:lat_count], grad_cond_part[lat_count:])
        kept = jnp.where(first, part_low, part_high)
        got = swap(jnp.where(first, part_high, part_low), "shard", 1)
        grad_cond_act = jnp.concatenate(
            [jnp.where(first, kept, got), jnp.where(first, got, kept)], 1
        )
    else:
        grad_cond_act = lax.all_to_all(
            grad_cond_part, "shard", split_axis=0, concat_axis=1, tiled=True
        )
    grad_condition = jax.vjp(silu_act, cond_float)[1](grad_cond_act)[0]

    def pick(values, start, size, axis):
        part = size // shard_count
        return lax.dynamic_slice_in_dim(values, start + shard_at * part, part, axis)

    bias_width = head_local * 2 * head_size
    hidden = grad_up_bias.shape[0]
    qv_sum = bias_all[:bias_width].reshape(head_local, 2 * head_size)
    summed = (
        lax.psum(scatter_shard(grad_qkv_weight, 0).astype(jnp.bfloat16), "ctx")
        .astype(jnp.float32)
        .reshape(stored, head_local, 3 * head_size),
        pick(qv_sum, 0, 2 * head_size, 1),
        lax.psum(scatter_shard(grad_out_weight, 1).astype(jnp.bfloat16), "ctx").astype(jnp.float32),
        pick(bias_all, bias_width, model_width, 0),
        lax.psum(scatter_shard(grad_up_weight, 0).astype(jnp.bfloat16), "ctx").astype(jnp.float32),
        pick(bias_all, bias_width + model_width, hidden, 0),
        lax.psum(scatter_shard(grad_down_weight, 1).astype(jnp.bfloat16), "ctx").astype(
            jnp.float32
        ),
        pick(bias_all, bias_width + model_width + hidden, model_width, 0),
    )
    return (
        result,
        grad_tokens,
        grad_condition,
        grad_ada_weight,
        grad_ada_bias,
        summed[0],
        summed[1],
        summed[2],
        summed[3],
        summed[4],
        summed[5],
        summed[6],
        summed[7],
    )


def solution(mesh):
    return jax.shard_map(
        local,
        mesh=mesh,
        in_specs=(
            P("shard", "ctx", None),
            P("shard", None),
            P("shard", None),
            P(),
            P("shard", "tp", None),
            P("tp", None),
            P("tp", "shard"),
            P(),
            P("shard", "tp"),
            P("tp"),
            P("tp", "shard"),
            P(),
            P("shard", "ctx", None),
        ),
        out_specs=(
            P("shard", "ctx", None),
            P("shard", "ctx", None),
            P("shard", None),
            P("shard", None),
            P("shard"),
            P("shard", "tp", None),
            P("tp", "shard"),
            P("tp", "shard"),
            P("shard"),
            P("shard", "tp"),
            P(("tp", "shard")),
            P("tp", "shard"),
            P("shard"),
        ),
        check_vma=False,
    )
```

profile of v0, /device:TPU:0, one launch (start us, length us, event | category | flops | bytes accessed | tf_op | source)
XLA Modules:
  0.0 635.3 jit_solution(15593193496477154573)
XLA Ops:
  8.1 3.0 collective-permute-start
  16.5 4.4 fusion.83
  21.0 2.1 collective-permute-start.1
  23.2 16.3 %collective-permute-done.1 = f32[3,6912]{1,0:T(4,128)S(1)} collective-permute-done((f32[3,6912]{1,0:T(4,128)S(1)}, f32[3,6912]{1,0:T(4,128)S(1)}, u32[]{:S(2)}, u32[]{:S(2)}) %collective-permute-start.1) | collective-permute-done | bytes 82976 | tf_op jit(solution)/shard_map/ppermute | solution.py:96
  40.9 2.5 fusion.40
  46.3 2.3 copy.168
  48.7 4.0 add_convert_fusion.4
  53.8 4.9 all-to-all-start
  61.3 2.2 fusion.34
  63.5 25.8 %all-to-all-done = bf16[3,256,4,216]{1,3,0,2:T(8,128)(2,1)S(1)} async-done(((bf16[3,256,4,216]{1,3,0,2:T(8,128)(2,1)}), bf16[3,256,4,216]{1,3,0,2:T(8,128)(2,1)S(1)}, u32[]{:S(2)}, u32[]{:S(2)}) %all-to-all-start) | async-done | bytes 1327136 | tf_op jit(solution)/shard_map/all_to_all | solution.py:197
  89.5 9.3 %while.22 = (s32[]{:T(128)}, bf16[3,1024,1,72]{1,3,2,0:T(8,128)(2,1)S(1)}, f32[3,1,1024]{2,1,0:T(1,128)}, bf16[3,1024,1,216]{1,3,2,0:T(8,128)(2,1)S(1)}, s32[]{:T(128)}) while((s32[]{:T(128)}, bf16[3,1024,1,72]{1,3,2,0:T(8,128)(2,1)S(1)}, f32[3,1,1024]{2,1,0:T(1,128)}, bf16[3,1024,1,216]{1,3,2,0:T(8,128)(2,1)S(1)}, s32[]{:T(128)}) %tuple.107), condition=%wide.region_5.6_spmd, body=%wide.region_2.5_spmd.sunk | while | flops 311499776 | bytes 14098513 | solution.py:62
  99.5 2.2 reshape.412
  101.7 3.5 all-to-all-start.1
  107.9 9.5 %all-to-all-done.1 = bf16[4,2,27648]{2,1,0:T(2,128)(2,1)S(1)} async-done(((bf16[4,2,27648]{2,1,0:T(2,128)(2,1)}), bf16[4,2,27648]{2,1,0:T(2,128)(2,1)S(1)}, u32[]{:S(2)}, u32[]{:S(2)}) %all-to-all-start.1) | async-done | bytes 442400 | tf_op jit(solution)/shard_map/all_to_all | solution.py:199
  121.0 2.4 convolution_convert_fusion.3
  123.6 3.1 broadcast_select_fusion.3
  126.7 3.2 broadcast_select_fusion.1
  129.9 38.0 %all-reduce.7.cloned.1.call-done = bf16[768,1152]{1,0:T(8,128)(2,1)} async-done(((bf16[768,1152]{1,0:T(8,128)(2,1)}), bf16[768,1152]{1,0:T(8,128)(2,1)}) %all-reduce.7.cloned.1.call-update) | async-done | bytes 1769488 | tf_op jit(solution)/shard_map/psum | solution.py:203
  167.9 1.8 convert_add_fusion.3
  173.8 2.7 convolution_add_fusion
  176.5 5.0 fusion.86
  181.5 6.9 %fusion.94 = (f32[1152]{0:T(1024)}, bf16[768,1152]{1,0:T(8,128)(2,1)S(1)}) fusion(f32[768,1152]{1,0:T(8,128)S(1)} %convolution_add_fusion, bf16[768,1152]{1,0:T(8,128)(2,1)S(1)} %bitcast.203, bf16[1152,576]{0,1:T(8,128)(2,1)S(1)} %copy-done.29, bf16[1152,576]{0,1:T(8,128)(2,1)S(1)} %copy-done.28), kind=kOutput, calls=%fused_computation.200 | convolution fusion | flops 2065857408 | bytes 9736704 | tf_op jit(solution)/shard_map/dot_general | solution.py:37
  188.4 3.8 convolution_convert_fusion.1
  192.3 4.0 select_convert_fusion
  197.8 4.9 fusion.60
  202.6 35.9 %all-reduce.9.cloned.1.call-done = bf16[3,256,1152]{2,1,0:T(8,128)(2,1)} async-done(((bf16[3,256,1152]{2,1,0:T(8,128)(2,1)}), bf16[3,256,1152]{2,1,0:T(8,128)(2,1)}) %all-reduce.9.cloned.1.call-update) | async-done | bytes 1769488 | tf_op jit(solution)/shard_map/psum | solution.py:239
  238.5 2.3 fusion.41
  240.9 2.4 fusion.50
  243.3 2.9 multiply_reduce_fusion.4
  251.2 2.2 reshape.363
  253.4 1.9 copy.175
  255.3 4.8 all-to-all-start.2
  260.1 7.2 %convolution_convert_fusion.2 = bf16[768,1152]{1,0:T(8,128)(2,1)} fusion(bf16[1152,576]{0,1:T(8,128)(2,1)} %get-tuple-element.192, bf16[1152,576]{0,1:T(8,128)(2,1)} %get-tuple-element.191, f32[768,1152]{1,0:T(8,128)} %copy-done.70), kind=kOutput, calls=%fused_computation.96 | convolution fusion | flops 2052587520 | bytes 7962624 | tf_op jit(solution)/shard_map/dot_general | solution.py:220
  267.3 5.6 all-to-all-done.2
  272.8 1.8 copy.198
  274.6 23.0 %while.23 = (s32[]{:T(128)}, bf16[3,1024,1,216]{1,3,2,0:T(8,128)(2,1)}, bf16[3,1024,1,216]{1,3,2,0:T(8,128)(2,1)}, f32[3,1,1024]{2,1,0:T(1,128)}, bf16[3,1024,1,72]{1,3,2,0:T(8,128)(2,1)}, /*index=5*/s32[]{:T(128)}) while((s32[]{:T(128)}, bf16[3,1024,1,216]{1,3,2,0:T(8,128)(2,1)}, bf16[3,1024,1,216]{1,3,2,0:T(8,128)(2,1)}, ...), condition=%wide.region_15.16_spmd, body=%wide.region_13.15_spmd.sunk | while | flops 769252352 | bytes 36499580 | solution.py:257
  297.7 4.1 copy.179
  301.8 4.5 all-to-all-start.3
  306.3 2.4 fusion.96
  310.4 3.9 select_convert_fusion.1
  316.6 3.8 collective-permute-done.11
  321.4 4.4 add_convert_fusion.2
  325.8 28.2 %all-to-all-done.3 = bf16[3,1024,1,216]{3,0,2,1:T(4,128)(2,1)} async-done(((bf16[3,1024,1,216]{3,0,2,1:T(4,128)(2,1)}), bf16[3,1024,1,216]{3,0,2,1:T(4,128)(2,1)}, u32[]{:S(2)}, u32[]{:S(2)}) %all-to-all-start.3) | async-done | bytes 1327136 | tf_op jit(solution)/shard_map/all_to_all | solution.py:258
  354.0 4.5 copy.190
  358.5 4.1 copy.181
  362.6 4.2 reshape.364
  366.8 5.3 convolution_convert_fusion
  372.2 4.5 add_convert_fusion.3
  380.4 4.0 fusion.95
  384.4 2.0 copy-done.15
  389.0 56.7 %all-reduce.11.cloned.1.call-done = (bf16[768,1152]{1,0:T(8,128)(2,1)}, bf16[3,256,1152]{2,1,0:T(8,128)(2,1)}) async-done(((bf16[768,1152]{1,0:T(8,128)(2,1)}, bf16[3,256,1152]{2,1,0:T(8,128)(2,1)}), (bf16[768,1152]{1,0:T(8,128)(2,1)}, bf16[3,256,1152]{2,1,0:T(8,128)(2,1)})) %all-reduce.11.cloned.1.call-update) | async-done | bytes 3538960 | tf_op jit(solution)/shard_map/psum | solution.py:219
  445.7 3.0 fusion.46
  448.8 2.7 fusion.51
  453.0 2.8 fusion.33
  459.7 3.7 add_convert_fusion.5
  463.4 2.5 copy.186
  466.9 2.5 collective-permute-start.7
  470.0 8.2 %collective-permute-done.7 = f32[24768]{0:T(1024)S(1)} collective-permute-done((f32[24768]{0:T(1024)S(1)}, f32[24768]{0:T(1024)S(1)}, u32[]{:S(2)}, u32[]{:S(2)}) %collective-permute-start.7) | collective-permute-done | bytes 99104 | tf_op jit(solution)/shard_map/ppermute | solution.py:96
  479.8 4.1 add_add_fusion.2
  486.5 5.5 fusion.64
  493.3 8.2 %fusion.63 = f32[576,6912]{1,0:T(8,128)} fusion(bf16[3,6912]{1,0:T(4,128)(2,1)S(1)} %get-tuple-element.202, bf16[3,6912]{1,0:T(4,128)(2,1)S(1)} %get-tuple-element.200, s32[]{:T(128)S(6)} %select_n.170, bf16[3,1152]{1,0:T(4,128)(2,1)S(1)} %copy-done.51, bf16[3,1152]{1,0:T(4,128)(2,1)S(1)} %copy-done.49), kind=kOutput, calls=%fused_computation.137 | convolution fusion | flops 47955456 | bytes 16022020 | tf_op jit(solution)/shard_map/dot_general | solution.py:31
  502.9 117.2 %all-reduce.13.cloned.1.call-done = (bf16[576,4,216]{0,2,1:T(8,128)(2,1)}, bf16[288,576]{1,0:T(8,128)(2,1)}, bf16[576,1152]{1,0:T(8,128)(2,1)}, bf16[1152,576]{0,1:T(8,128)(2,1)}) async-done(((bf16[576,4,216]{0,2,1:T(8,128)(2,1)}, bf16[288,576]{1,0:T(8,128)(2,1)}, bf16[576,1152]{1,0:T(8,128)(2,1)}, bf16[1152,576]{0,1:T(8,128)(2,1)}), (bf16[576,4,216]{0,2,1:T(8,128)(2,1)}, bf16[288,576]{1,0:T(8,128)(2,1)}, ...) | async-done | bytes 3981328 | tf_op jit(solution)/shard_map/psum | solution.py:332
  620.1 2.0 convert_element_type.167
  622.1 2.8 reshape.375
  (303 shorter events, 93.1 us)
Async XLA Ops:
  7.2 8.7 %copy-start.52 = (bf16[3,1152]{1,0:T(4,128)(2,1)S(1)}, bf16[3,1152]{1,0:T(4,128)(2,1)}, u32[]{:S(2)}) copy-start(bf16[3,1152]{1,0:T(4,128)(2,1)} %param.18) | copy-start | bytes 20740
  7.2 7.5 %copy-start = (bf16[3,256,1152]{2,1,0:T(8,128)(2,1)S(1)}, bf16[3,256,1152]{2,1,0:T(8,128)(2,1)}, u32[]{:S(2)}) copy-start(bf16[3,256,1152]{2,1,0:T(8,128)(2,1)} %param.17) | copy-start | bytes 5308420
  7.2 8.1 %copy-start.68 = (f32[4,144]{1,0:T(4,128)S(1)}, f32[4,144]{1,0:T(4,128)}, u32[]{:S(2)}) copy-start(f32[4,144]{1,0:T(4,128)} %param.22) | copy-start | bytes 6916
  8.1 7.8 %collective-permute-start = (bf16[3,1152]{1,0:T(4,128)(2,1)S(1)}, bf16[3,1152]{1,0:T(4,128)(2,1)S(1)}, u32[]{:S(2)}, u32[]{:S(2)}) collective-permute-start(bf16[3,1152]{1,0:T(4,128)(2,1)S(1)} %fusion.68), channel_id=1, source_target_pairs={{0,16},{16,0},{1,17},{17,1},{2,18},{18,2},{3,19},{19,3},{4,20},{20... | collective-permute-start | bytes 20744 | tf_op jit(solution)/shard_map/ppermute | solution.py:96
  12.8 30.6 %collective-permute-start.2 = (bf16[576,864]{1,0:T(8,128)(2,1)S(1)}, bf16[576,864]{1,0:T(8,128)(2,1)}, u32[]{:S(2)}, u32[]{:S(2)}) collective-permute-start(bf16[576,864]{1,0:T(8,128)(2,1)S(1)} %copy.166), channel_id=1, source_target_pairs={{0,16},{16,0},{1,17},{17,1},{2,18},{18,2},{3,19},{19,3},{4,20},{20... | collective-permute-start | bytes 2985992 | tf_op jit(solution)/shard_map/ppermute | solution.py:96
  14.7 26.2 %copy-start.45 = (f32[3,256]{1,0:T(4,128)}, f32[3,256]{1,0:T(4,128)S(1)}, u32[]{:S(2)}) copy-start(f32[3,256]{1,0:T(4,128)S(1)} %broadcast_multiply_fusion.1) | copy-start | bytes 9220
  15.3 25.6 %copy-start.58 = (f32[3,256]{1,0:T(4,128)}, f32[3,256]{1,0:T(4,128)S(1)}, u32[]{:S(2)}) copy-start(f32[3,256]{1,0:T(4,128)S(1)} %fusion.72) | copy-start | bytes 9220
  16.5 22.9 %copy-start.64 = (f32[6912]{0:T(1024)S(1)}, f32[6912]{0:T(1024)}, u32[]{:S(2)}) copy-start(f32[6912]{0:T(1024)} %param.20) | copy-start | bytes 82948
  21.0 18.4 %collective-permute-start.1 = (f32[3,6912]{1,0:T(4,128)S(1)}, f32[3,6912]{1,0:T(4,128)S(1)}, u32[]{:S(2)}, u32[]{:S(2)}) collective-permute-start(f32[3,6912]{1,0:T(4,128)S(1)} %slice_select_fusion), channel_id=1, source_target_pairs={{0,16},{16,0},{1,17},{17,1},{2,18},{18,2},{3,19},{19,3},{4,20},{20... | collective-permute-start | bytes 248840 | tf_op jit(solution)/shard_map/ppermute | solution.py:96
  40.3 4.5 copy-start.34
  52.7 8.6 %copy-start.11 = (bf16[3,256,1152]{2,1,0:T(8,128)(2,1)S(1)}, bf16[3,256,1152]{2,1,0:T(8,128)(2,1)}, u32[]{:S(2)}) copy-start(bf16[3,256,1152]{2,1,0:T(8,128)(2,1)} %param.29) | copy-start | bytes 5308420
  53.8 35.5 %all-to-all-start = ((bf16[3,256,4,216]{1,3,0,2:T(8,128)(2,1)}), bf16[3,256,4,216]{1,3,0,2:T(8,128)(2,1)S(1)}, u32[]{:S(2)}, u32[]{:S(2)}) async-start(bf16[3,256,4,216]{1,3,0,2:T(8,128)(2,1)} %copy.169), calls=%async_computation | async-start | bytes 2654208 | tf_op jit(solution)/shard_map/all_to_all | solution.py:197
  58.7 48.0 %collective-permute-start.3 = (bf16[288,576]{1,0:T(8,128)(2,1)}, bf16[288,576]{1,0:T(8,128)(2,1)}, u32[]{:S(2)}, u32[]{:S(2)}) collective-permute-start(bf16[288,576]{1,0:T(8,128)(2,1)} %param.23), channel_id=1, source_target_pairs={{0,16},{16,0},{1,17},{17,1},{2,18},{18,2},{3,19},{19,3},{4,20},{20... | collective-permute-start | bytes 995336 | tf_op jit(solution)/shard_map/ppermute | solution.py:96
  59.2 64.3 %collective-permute-start.4 = (bf16[576,1152]{1,0:T(8,128)(2,1)}, bf16[576,1152]{1,0:T(8,128)(2,1)}, u32[]{:S(2)}, u32[]{:S(2)}) collective-permute-start(bf16[576,1152]{1,0:T(8,128)(2,1)} %param.25), channel_id=1, source_target_pairs={{0,16},{16,0},{1,17},{17,1},{2,18},{18,2},{3,19},{19,3},{4,20},{20... | collective-permute-start | bytes 3981320 | tf_op jit(solution)/shard_map/ppermute | solution.py:96
  60.7 66.0 %collective-permute-start.5 = (bf16[1152,576]{0,1:T(8,128)(2,1)}, bf16[1152,576]{0,1:T(8,128)(2,1)}, u32[]{:S(2)}, u32[]{:S(2)}) collective-permute-start(bf16[1152,576]{0,1:T(8,128)(2,1)} %param.27), channel_id=1, source_target_pairs={{0,16},{16,0},{1,17},{17,1},{2,18},{18,2},{3,19},{19,3},{4,20},{20... | collective-permute-start | bytes 3981320 | tf_op jit(solution)/shard_map/ppermute | solution.py:96
  98.8 21.0 %copy-start.7 = (bf16[3,1024,1,216]{1,3,2,0:T(8,128)(2,1)}, bf16[3,1024,1,216]{1,3,2,0:T(8,128)(2,1)S(1)}, u32[]{:S(2)}) copy-start(bf16[3,1024,1,216]{1,3,2,0:T(8,128)(2,1)S(1)} %get-tuple-element.340) | copy-start | bytes 3981316
  98.8 6.6 %copy-start.60 = (f32[3,1,1152]{2,1,0:T(1,128)S(1)}, f32[3,1,1152]{2,1,0:T(1,128)}, u32[]{:S(2)}) copy-start(f32[3,1,1152]{2,1,0:T(1,128)} %get-tuple-element.206) | copy-start | bytes 41476
  98.8 6.7 %copy-start.61 = (f32[3,1,1152]{2,1,0:T(1,128)S(1)}, f32[3,1,1152]{2,1,0:T(1,128)}, u32[]{:S(2)}) copy-start(f32[3,1,1152]{2,1,0:T(1,128)} %get-tuple-element.207) | copy-start | bytes 41476
  101.7 15.7 %all-to-all-start.1 = ((bf16[4,2,27648]{2,1,0:T(2,128)(2,1)}), bf16[4,2,27648]{2,1,0:T(2,128)(2,1)S(1)}, u32[]{:S(2)}, u32[]{:S(2)}) async-start(bf16[4,2,27648]{2,1,0:T(2,128)(2,1)} %reshape.412), calls=%async_computation.1 | async-start | bytes 884736 | tf_op jit(solution)/shard_map/all_to_all | solution.py:199
  105.2 62.7 %all-reduce.7.cloned.1.call-start = ((), (), s32[]{:S(2)}) async-start(), calls=%async_computation.4 | async-start | bytes 3538944 | tf_op jit(solution)/shard_map/psum | solution.py:203
  107.9 15.6 %copy-start.38 = (bf16[288,576]{1,0:T(8,128)(2,1)}, bf16[288,576]{1,0:T(8,128)(2,1)S(1)}, u32[]{:S(2)}) copy-start(bf16[288,576]{1,0:T(8,128)(2,1)S(1)} %get-tuple-element.195) | copy-start | bytes 995332
  107.9 15.6 %copy-start.40 = (bf16[288,576]{1,0:T(8,128)(2,1)}, bf16[288,576]{1,0:T(8,128)(2,1)S(1)}, u32[]{:S(2)}) copy-start(bf16[288,576]{1,0:T(8,128)(2,1)S(1)} %get-tuple-element.196) | copy-start | bytes 995332
  119.8 3.8 copy-start.24
  123.5 3.3 copy-start.25
  123.5 115.0 %all-reduce.9.cloned.1.call-start = ((), (), s32[]{:S(2)}) async-start(), calls=%async_computation.5 | async-start | bytes 3538944 | tf_op jit(solution)/shard_map/psum | solution.py:239
  126.7 41.2 %copy-start.66 = (f32[1152]{0:T(1024)S(1)}, f32[1152]{0:T(1024)}, u32[]{:S(2)}) copy-start(f32[1152]{0:T(1024)} %param.24) | copy-start | bytes 13828
  176.5 5.0 copy-start.70
  176.5 5.0 copy-start.28
  176.5 5.0 copy-start.29
  188.4 3.8 copy-start.71
  192.2 5.5 copy-start.22
  192.3 5.5 copy-start.72
  196.3 125.1 %collective-permute-start.13 = (bf16[1152,576]{0,1:T(8,128)(2,1)}, bf16[1152,576]{0,1:T(8,128)(2,1)}, u32[]{:S(2)}, u32[]{:S(2)}) collective-permute-start(bf16[1152,576]{0,1:T(8,128)(2,1)} %select_convert_fusion), channel_id=1, source_target_pairs={{0,16},{16,0},{1,17},{17,1},{2,18},{18,2},{3,19},{19,3},{4,20},{20... | collective-permute-start | bytes 3981320 | tf_op jit(solution)/shard_map/ppermute | solution.py:96
  246.2 3.3 copy-start.39
  246.2 3.3 copy-start.41
  255.3 17.5 %all-to-all-start.2 = ((bf16[3,256,4,72]{1,3,0,2:T(8,128)(2,1)}), bf16[3,256,4,72]{1,3,0,2:T(8,128)(2,1)}, u32[]{:S(2)}, u32[]{:S(2)}) async-start(bf16[3,256,4,72]{1,3,0,2:T(8,128)(2,1)} %copy.175), calls=%async_computation.2 | async-start | bytes 884736 | tf_op jit(solution)/shard_map/all_to_all | solution.py:256
  301.8 52.2 %all-to-all-start.3 = ((bf16[3,1024,1,216]{3,0,2,1:T(4,128)(2,1)}), bf16[3,1024,1,216]{3,0,2,1:T(4,128)(2,1)}, u32[]{:S(2)}, u32[]{:S(2)}) async-start(bf16[3,1024,1,216]{3,0,2,1:T(4,128)(2,1)} %copy.179), calls=%async_computation.3 | async-start | bytes 4194304 | tf_op jit(solution)/shard_map/all_to_all | solution.py:258
  306.2 139.4 %all-reduce.11.cloned.1.call-start = ((), (), s32[]{:S(2)}) async-start(), calls=%async_computation.6 | async-start | bytes 7077888 | tf_op jit(solution)/shard_map/psum | solution.py:219
  308.6 6.2 copy-start.55
  308.7 6.8 %copy-start.56 = (f32[3,1152]{1,0:T(4,128)S(1)}, f32[3,1152]{1,0:T(4,128)}, u32[]{:S(2)}) copy-start(f32[3,1152]{1,0:T(4,128)} %get-tuple-element.152) | copy-start | bytes 41476
  308.7 7.4 %copy-start.54 = (f32[3,1152]{1,0:T(4,128)S(1)}, f32[3,1152]{1,0:T(4,128)}, u32[]{:S(2)}) copy-start(f32[3,1152]{1,0:T(4,128)} %get-tuple-element.155) | copy-start | bytes 41476
  308.8 11.6 %collective-permute-start.11 = (bf16[288,576]{1,0:T(8,128)(2,1)S(1)}, bf16[288,576]{1,0:T(8,128)(2,1)S(1)}, u32[]{:S(2)}, u32[]{:S(2)}) collective-permute-start(bf16[288,576]{1,0:T(8,128)(2,1)S(1)} %select_convert_fusion.3), channel_id=1, source_target_pairs={{0,16},{16,0},{1,17},{17,1},{2,18},{18,2},{3,19},{19,3},{4,20},{20... | collective-permute-start | bytes 995336 | tf_op jit(solution)/shard_map/ppermute | solution.py:96
  314.2 58.0 %collective-permute-start.12 = (bf16[576,1152]{1,0:T(8,128)(2,1)}, bf16[576,1152]{1,0:T(8,128)(2,1)}, u32[]{:S(2)}, u32[]{:S(2)}) collective-permute-start(bf16[576,1152]{1,0:T(8,128)(2,1)} %select_convert_fusion.1), channel_id=1, source_target_pairs={{0,16},{16,0},{1,17},{17,1},{2,18},{18,2},{3,19},{19,3},{4,20},{20... | collective-permute-start | bytes 3981320 | tf_op jit(solution)/shard_map/ppermute | solution.py:96
  372.2 248.0 %all-reduce.13.cloned.1.call-start = ((), (), s32[]{:S(2)}) async-start(), calls=%async_computation.7 | async-start | bytes 8257536 | tf_op jit(solution)/shard_map/psum | solution.py:332
  372.2 4.5 copy-start.14
  380.4 65.3 %copy-start.46 = (f32[3,256]{1,0:T(4,128)S(1)}, f32[3,256]{1,0:T(4,128)}, u32[]{:S(2)}) copy-start(f32[3,256]{1,0:T(4,128)} %copy-done.45) | copy-start | bytes 9220
  386.4 62.3 %copy-start.63 = (f32[3,256]{1,0:T(4,128)S(1)}, f32[3,256]{1,0:T(4,128)}, u32[]{:S(2)}) copy-start(f32[3,256]{1,0:T(4,128)} %copy-done.62) | copy-start | bytes 9220
  386.4 62.3 %copy-start.59 = (f32[3,256]{1,0:T(4,128)S(1)}, f32[3,256]{1,0:T(4,128)}, u32[]{:S(2)}) copy-start(f32[3,256]{1,0:T(4,128)} %copy-done.58) | copy-start | bytes 9220
  387.5 72.1 %collective-permute-start.10 = (bf16[576,864]{1,0:T(8,128)(2,1)}, bf16[576,864]{1,0:T(8,128)(2,1)}, u32[]{:S(2)}, u32[]{:S(2)}) collective-permute-start(bf16[576,864]{1,0:T(8,128)(2,1)} %select_convert_fusion.2), channel_id=1, source_target_pairs={{0,16},{16,0},{1,17},{17,1},{2,18},{18,2},{3,19},{19,3},{4,20},{20... | collective-permute-start | bytes 2985992 | tf_op jit(solution)/shard_map/ppermute | solution.py:96
  445.7 7.0 %copy-start.23 = (bf16[768,1152]{1,0:T(8,128)(2,1)S(1)}, bf16[768,1152]{1,0:T(8,128)(2,1)}, u32[]{:S(2)}) copy-start(bf16[768,1152]{1,0:T(8,128)(2,1)} %get-tuple-element.175) | copy-start | bytes 5308420
  445.7 7.0 %copy-start.67 = (f32[1152]{0:T(1024)S(1)}, f32[1152]{0:T(1024)}, u32[]{:S(2)}) copy-start(f32[1152]{0:T(1024)} %param.28) | copy-start | bytes 13828
  453.0 3.7 copy-start.65
  458.2 7.7 %collective-permute-start.6 = (f32[24768]{0:T(1024)}, f32[24768]{0:T(1024)}, u32[]{:S(2)}, u32[]{:S(2)}) collective-permute-start(f32[24768]{0:T(1024)} %concatenate.57), channel_id=1, source_target_pairs={{0,4},{4,0},{8,12},{12,8},{1,5},{5,1},{9,13},{13,9},{2,6},{6,2},{1... | collective-permute-start | bytes 297224 | tf_op jit(solution)/shard_map/ppermute | solution.py:96
  463.4 16.4 %copy-start.3 = (bf16[3,256,1152]{2,1,0:T(8,128)(2,1)S(1)}, bf16[3,256,1152]{2,1,0:T(8,128)(2,1)}, u32[]{:S(2)}) copy-start(bf16[3,256,1152]{2,1,0:T(8,128)(2,1)} %param.17) | copy-start | bytes 5308420
  463.4 16.4 %copy-start.9 = (bf16[3,256,1152]{2,1,0:T(8,128)(2,1)S(1)}, bf16[3,256,1152]{2,1,0:T(8,128)(2,1)}, u32[]{:S(2)}) copy-start(bf16[3,256,1152]{2,1,0:T(8,128)(2,1)} %get-tuple-element.176) | copy-start | bytes 5308420
  466.9 11.4 %collective-permute-start.7 = (f32[24768]{0:T(1024)S(1)}, f32[24768]{0:T(1024)S(1)}, u32[]{:S(2)}, u32[]{:S(2)}) collective-permute-start(f32[24768]{0:T(1024)S(1)} %add.234), channel_id=1, source_target_pairs={{0,8},{4,12},{8,0},{12,4},{1,9},{5,13},{9,1},{13,5},{2,10},{6,14},... | collective-permute-start | bytes 297224 | tf_op jit(solution)/shard_map/ppermute | solution.py:96
  478.2 5.6 copy-start.37
  478.2 5.6 collective-permute-start.8
  486.5 6.9 %copy-start.49 = (bf16[3,1152]{1,0:T(4,128)(2,1)S(1)}, bf16[3,1152]{1,0:T(4,128)(2,1)}, u32[]{:S(2)}) copy-start(bf16[3,1152]{1,0:T(4,128)(2,1)} %copy-done.48) | copy-start | bytes 20740
  486.5 6.9 %copy-start.51 = (bf16[3,1152]{1,0:T(4,128)(2,1)S(1)}, bf16[3,1152]{1,0:T(4,128)(2,1)}, u32[]{:S(2)}) copy-start(bf16[3,1152]{1,0:T(4,128)(2,1)} %copy-done.50) | copy-start | bytes 20740
  492.0 10.3 %collective-permute-start.9 = (f32[3,576]{1,0:T(4,128)S(1)}, f32[3,576]{1,0:T(4,128)S(1)}, u32[]{:S(2)}, u32[]{:S(2)}) collective-permute-start(f32[3,576]{1,0:T(4,128)S(1)} %slice_select_fusion.3), channel_id=1, source_target_pairs={{0,16},{16,0},{1,17},{17,1},{2,18},{18,2},{3,19},{19,3},{4,20},{20... | collective-permute-start | bytes 20744 | tf_op jit(solution)/shard_map/ppermute | solution.py:96
  493.3 8.9 %copy-start.53 = (bf16[3,1152]{1,0:T(4,128)(2,1)S(1)}, bf16[3,1152]{1,0:T(4,128)(2,1)}, u32[]{:S(2)}) copy-start(bf16[3,1152]{1,0:T(4,128)(2,1)} %param.18) | copy-start | bytes 20740
  620.1 4.9 copy-start.27
  622.1 4.5 copy-start.26
  (33 other events, 60.5 us)
Sparse Core Ops, SparseCore 0:
  123.6 44.2 all-reduce.6
  192.4 46.0 all-reduce.8
  372.3 73.3 all-reduce.10
  466.0 154.0 all-reduce.12
where the time goes:
time: 644 us; the launch traced here: 635 us
  waiting for transfers between devices  345 us (54%)
  other arithmetic  86.8 us (13%)
  matrix products  85 us (13%)
  local copies, waits for them, and re-layouts  66.3 us (10%)
  starting transfers between devices  36.9 us (6%)
  between operations  15.1 us (2%)
    psum x1, waiting for transfers between devices, local(): lax.psum(scatter_shard(grad_qkv_weight, 0).astype(jnp.bfloat16), 'ctx')  117 us
    psum x1, waiting for transfers between devices, local(): lax.psum(jnp.dot(activated, down_full, preferred_element_type=jnp.float32...  56.7 us
    psum x1, waiting for transfers between devices, local(): lax.psum(jnp.dot(attn_rows, out_full, preferred_element_type=jnp.float32)...  38 us
    psum x1, waiting for transfers between devices, local(): lax.psum(contract_cols(grad_up_low, up_full).astype(jnp.bfloat16), 'tp')  35.9 us
    ppermute x14, waiting for transfers between devices, swap(): return lax.ppermute(values, axis, [(i, i ^ distance) for i in range(count)])  28.3 us
    all_to_all x1, waiting for transfers between devices, local(): lax.all_to_all(grad_packed_heads, 'ctx', split_axis=1, concat_axis=2, til...  28.2 us
    all_to_all x1, waiting for transfers between devices, local(): lax.all_to_all(packed, 'ctx', split_axis=2, concat_axis=1, tiled=True)  25.8 us
    dot_general x5, matrix products, contract_rows(): lax.dot_general(left, right, (((0,), (0,)), ((), ())), preferred_element_...  24.4 us
  transfers between devices with their start and end apart: 22, of which 11 were waited for; matrix products, arithmetic and copies ran while one was open for 29% of the time, Pallas kernels for 0%

commit v1 on v0

--- a/solution.py
+++ b/solution.py
@@ -1,7 +1,23 @@
+import functools
 import jax
 import jax.numpy as jnp
 from jax import lax
 from jax.sharding import PartitionSpec as P
+
+
+def link_slot(message, which_axis, along_dim, k_dim):
+    return jnp.concatenate(
+        lax.all_to_all(
+            jnp.stack(jnp.split(message, lax.axis_size(which_axis), axis=along_dim)),
+            which_axis,
+            0,
+            0,
+        ),
+        axis=k_dim,
+    )
+
+
+_set_forms = functools.partial(link_slot, which_axis="ctx", along_dim=1, k_dim=2)
 
 
 def layer_norm(values):
@@ -255,7 +271,7 @@
     )
     grad_heads = lax.all_to_all(grad_attended, "ctx", split_axis=2, concat_axis=1, tiled=True)
     grad_packed_heads = lax.map(attend_backward, (head_packed, log_total, grad_heads))
-    grad_packed = lax.all_to_all(grad_packed_heads, "ctx", split_axis=1, concat_axis=2, tiled=True)
+    grad_packed = _set_forms(grad_packed_heads)
     bias_sums = jnp.sum(grad_packed.astype(jnp.float32), (0, 1))
     grad_qv_bias = jnp.concatenate([bias_sums[:, :head_size], bias_sums[:, 2 * head_size :]], 1)
     grad_packed_rows = grad_packed.reshape(row_count, head_local * 3 * head_size)

time: 644 us -> 622 us (0.966)
  waiting for transfers between devices: 345 us -> 330 us
  local copies, waits for them, and re-layouts: 66.3 us -> 57.4 us
    all_to_all x1, waiting for transfers between devices: 28.2 us -> 11.7 us  [link_slot(): lax.all_to_all(jnp.stack(jnp.split(message, lax.axis_size(which_axis), ax...]
    all_to_all x2 -> x0, local copies, waits for them, and re-layouts: 8.61 us -> none  [local(): lax.all_to_all(grad_packed_heads, 'ctx', split_axis=1, concat_axis=2, til...]
    another operation x0 -> x3, local copies, waits for them, and re-layouts: none -> 6.44 us  [the longest x1 4.19 us: local(): grad_packed.reshape(row_count, head_local * 3 * head_size)]
    unnamed x151 -> x149, local copies, waits for them, and re-layouts: 16.6 us -> 16.6 us
where the time goes in v1:
time: 622 us; the launch traced here: 613 us
  waiting for transfers between devices  330 us (53%)
  other arithmetic  88.9 us (14%)
  matrix products  84.8 us (14%)
  local copies, waits for them, and re-layouts  57.4 us (9%)
  starting transfers between devices  36.9 us (6%)
  between operations  14.9 us (2%)
    psum x1, waiting for transfers between devices, local(): lax.psum(scatter_shard(grad_qkv_weight, 0).astype(jnp.bfloat16), 'ctx')  117 us
    psum x1, waiting for transfers between devices, local(): lax.psum(jnp.dot(activated, down_full, preferred_element_type=jnp.float32...  58 us
    psum x1, waiting for transfers between devices, local(): lax.psum(jnp.dot(attn_rows, out_full, preferred_element_type=jnp.float32)...  38 us
    psum x1, waiting for transfers between devices, local(): lax.psum(contract_cols(grad_up_low, up_full).astype(jnp.bfloat16), 'tp')  35.9 us
    ppermute x14, waiting for transfers between devices, swap(): return lax.ppermute(values, axis, [(i, i ^ distance) for i in range(count)])  28.3 us
    all_to_all x1, waiting for transfers between devices, local(): lax.all_to_all(packed, 'ctx', split_axis=2, concat_axis=1, tiled=True)  25.8 us
    dot_general x5, matrix products, contract_rows(): lax.dot_general(left, right, (((0,), (0,)), ((), ())), preferred_element_...  24.4 us
    dot_general x5, matrix products, contract_cols(): lax.dot_general(left, right, (((1,), (1,)), ((), ())), preferred_element_...  22.9 us
  transfers between devices with their start and end apart: 22, of which 11 were waited for; matrix products, arithmetic and copies ran while one was open for 29% of the time, Pallas kernels for 0%

profile of v1, /device:TPU:0, one launch (start us, length us, event | category | flops | bytes accessed | tf_op | source)
XLA Modules:
  0.0 613.0 jit_solution(12064170970771255064)
XLA Ops:
  8.1 3.0 collective-permute-start
  12.9 1.8 convert_reduce_fusion.2
  16.5 4.4 fusion.83
  21.0 2.1 collective-permute-start.1
  23.2 16.3 %collective-permute-done.1 = f32[3,6912]{1,0:T(4,128)S(1)} collective-permute-done((f32[3,6912]{1,0:T(4,128)S(1)}, f32[3,6912]{1,0:T(4,128)S(1)}, u32[]{:S(2)}, u32[]{:S(2)}) %collective-permute-start.1) | collective-permute-done | bytes 82976 | tf_op jit(solution)/shard_map/ppermute | solution.py:112
  40.9 2.5 fusion.40
  46.3 2.3 copy.137
  48.7 4.0 add_convert_fusion.4
  53.8 4.9 all-to-all-start
  61.3 2.2 fusion.34
  63.5 25.8 %all-to-all-done = bf16[3,256,4,216]{1,3,0,2:T(8,128)(2,1)S(1)} async-done(((bf16[3,256,4,216]{1,3,0,2:T(8,128)(2,1)}), bf16[3,256,4,216]{1,3,0,2:T(8,128)(2,1)S(1)}, u32[]{:S(2)}, u32[]{:S(2)}) %all-to-all-start) | async-done | bytes 1327136 | tf_op jit(solution)/shard_map/all_to_all | solution.py:213
  89.5 9.3 %while.22 = (s32[]{:T(128)}, bf16[3,1024,1,72]{1,3,2,0:T(8,128)(2,1)S(1)}, f32[3,1,1024]{2,1,0:T(1,128)}, bf16[3,1024,1,216]{1,3,2,0:T(8,128)(2,1)S(1)}, s32[]{:T(128)}) while((s32[]{:T(128)}, bf16[3,1024,1,72]{1,3,2,0:T(8,128)(2,1)S(1)}, f32[3,1,1024]{2,1,0:T(1,128)}, bf16[3,1024,1,216]{1,3,2,0:T(8,128)(2,1)S(1)}, s32[]{:T(128)}) %tuple.105), condition=%wide.region_5.6_spmd, body=%wide.region_2.5_spmd.sunk | while | flops 311499776 | bytes 14098513 | solution.py:78
  99.5 2.2 reshape.412
  101.7 3.5 all-to-all-start.1
  107.8 9.5 %all-to-all-done.1 = bf16[4,2,27648]{2,1,0:T(2,128)(2,1)S(1)} async-done(((bf16[4,2,27648]{2,1,0:T(2,128)(2,1)}), bf16[4,2,27648]{2,1,0:T(2,128)(2,1)S(1)}, u32[]{:S(2)}, u32[]{:S(2)}) %all-to-all-start.1) | async-done | bytes 442400 | tf_op jit(solution)/shard_map/all_to_all | solution.py:215
  121.1 2.4 convolution_convert_fusion.3
  123.6 3.1 broadcast_select_fusion.3
  126.7 3.2 broadcast_select_fusion.1
  129.9 38.0 %all-reduce.7.cloned.1.call-done = bf16[768,1152]{1,0:T(8,128)(2,1)} async-done(((bf16[768,1152]{1,0:T(8,128)(2,1)}), bf16[768,1152]{1,0:T(8,128)(2,1)}) %all-reduce.7.cloned.1.call-update) | async-done | bytes 1769488 | tf_op jit(solution)/shard_map/psum | solution.py:219
  167.9 1.8 convert_add_fusion.3
  173.8 2.7 convolution_add_fusion
  176.5 5.0 fusion.86
  181.5 6.7 %fusion.94 = (f32[1152]{0:T(1024)}, bf16[768,1152]{1,0:T(8,128)(2,1)S(1)}) fusion(f32[768,1152]{1,0:T(8,128)S(1)} %convolution_add_fusion, bf16[768,1152]{1,0:T(8,128)(2,1)S(1)} %bitcast.212, bf16[1152,576]{0,1:T(8,128)(2,1)S(1)} %copy-done.28, bf16[1152,576]{0,1:T(8,128)(2,1)S(1)} %copy-done.27), kind=kOutput, calls=%fused_computation.205 | convolution fusion | flops 2065857408 | bytes 9736704 | tf_op jit(solution)/shard_map/dot_general | solution.py:53
  188.2 3.8 convolution_convert_fusion.1
  192.1 4.0 select_convert_fusion
  197.6 4.9 fusion.60
  202.4 35.9 %all-reduce.9.cloned.1.call-done = bf16[3,256,1152]{2,1,0:T(8,128)(2,1)} async-done(((bf16[3,256,1152]{2,1,0:T(8,128)(2,1)}), bf16[3,256,1152]{2,1,0:T(8,128)(2,1)}) %all-reduce.9.cloned.1.call-update) | async-done | bytes 1769488 | tf_op jit(solution)/shard_map/psum | solution.py:255
  238.3 2.3 fusion.41
  240.7 2.4 fusion.50
  243.1 2.9 multiply_reduce_fusion.4
  246.0 1.8 copy-done.4
  251.0 2.2 reshape.363
  253.2 1.9 copy.144
  255.1 5.0 all-to-all-start.2
  260.1 7.2 %convolution_convert_fusion.2 = bf16[768,1152]{1,0:T(8,128)(2,1)} fusion(bf16[1152,576]{0,1:T(8,128)(2,1)} %get-tuple-element.174, bf16[1152,576]{0,1:T(8,128)(2,1)} %get-tuple-element.173, f32[768,1152]{1,0:T(8,128)} %copy-done.69), kind=kOutput, calls=%fused_computation.96 | convolution fusion | flops 2052587520 | bytes 7962624 | tf_op jit(solution)/shard_map/dot_general | solution.py:236
  267.3 5.6 all-to-all-done.2
  272.8 1.8 copy.165
  274.7 23.1 %while.23 = (s32[]{:T(128)}, bf16[3,1024,1,216]{1,3,2,0:T(8,128)(2,1)}, bf16[3,1024,1,216]{1,3,2,0:T(8,128)(2,1)}, f32[3,1,1024]{2,1,0:T(1,128)}, bf16[3,1024,1,72]{1,3,2,0:T(8,128)(2,1)}, /*index=5*/s32[]{:T(128)}) while((s32[]{:T(128)}, bf16[3,1024,1,216]{1,3,2,0:T(8,128)(2,1)}, bf16[3,1024,1,216]{1,3,2,0:T(8,128)(2,1)}, ...), condition=%wide.region_15.16_spmd, body=%wide.region_13.15_spmd.sunk | while | flops 769252352 | bytes 36499580 | solution.py:273
  301.2 4.3 all-to-all-start.3
  305.5 2.4 fusion.96
  309.6 3.9 select_convert_fusion.1
  315.9 3.8 collective-permute-done.11
  320.7 4.4 add_convert_fusion.2
  325.1 11.7 %all-to-all-done.3 = bf16[4,3,256,1,216]{2,4,1,3,0:T(8,128)(2,1)} async-done(((bf16[4,3,256,1,216]{2,4,1,3,0:T(8,128)(2,1)}), bf16[4,3,256,1,216]{2,4,1,3,0:T(8,128)(2,1)}, u32[]{:S(2)}, u32[]{:S(2)}) %all-to-all-start.3) | async-done | bytes 1327136 | tf_op jit(solution)/shard_map/all_to_all | solution.py:10
  336.8 3.8 copy.151
  340.6 4.2 reshape_reshape.3
  344.7 5.3 convolution_convert_fusion
  350.2 4.4 add_convert_fusion.3
  357.0 3.9 fusion.95
  360.9 2.0 copy-done.14
  365.6 58.0 %all-reduce.11.cloned.1.call-done = (bf16[768,1152]{1,0:T(8,128)(2,1)}, bf16[3,256,1152]{2,1,0:T(8,128)(2,1)}) async-done(((bf16[768,1152]{1,0:T(8,128)(2,1)}, bf16[3,256,1152]{2,1,0:T(8,128)(2,1)}), (bf16[768,1152]{1,0:T(8,128)(2,1)}, bf16[3,256,1152]{2,1,0:T(8,128)(2,1)})) %all-reduce.11.cloned.1.call-update) | async-done | bytes 3538960 | tf_op jit(solution)/shard_map/psum | solution.py:235
  423.7 3.0 fusion.46
  426.7 2.7 fusion.51
  430.9 2.8 fusion.33
  437.6 3.7 add_convert_fusion.5
  441.3 2.5 copy.154
  444.8 2.5 collective-permute-start.7
  447.9 8.2 %collective-permute-done.7 = f32[24768]{0:T(1024)S(1)} collective-permute-done((f32[24768]{0:T(1024)S(1)}, f32[24768]{0:T(1024)S(1)}, u32[]{:S(2)}, u32[]{:S(2)}) %collective-permute-start.7) | collective-permute-done | bytes 99104 | tf_op jit(solution)/shard_map/ppermute | solution.py:112
  457.7 4.1 add_add_fusion.2
  464.4 5.5 fusion.64
  471.2 8.2 %fusion.63 = f32[576,6912]{1,0:T(8,128)} fusion(bf16[3,6912]{1,0:T(4,128)(2,1)S(1)} %get-tuple-element.187, bf16[3,6912]{1,0:T(4,128)(2,1)S(1)} %get-tuple-element.185, s32[]{:T(128)S(6)} %select_n.170, bf16[3,1152]{1,0:T(4,128)(2,1)S(1)} %copy-done.50, bf16[3,1152]{1,0:T(4,128)(2,1)S(1)} %copy-done.48), kind=kOutput, calls=%fused_computation.142 | convolution fusion | flops 47955456 | bytes 16022020 | tf_op jit(solution)/shard_map/dot_general | solution.py:47
  480.8 117.2 %all-reduce.13.cloned.1.call-done = (bf16[576,4,216]{0,2,1:T(8,128)(2,1)}, bf16[288,576]{1,0:T(8,128)(2,1)}, bf16[576,1152]{1,0:T(8,128)(2,1)}, bf16[1152,576]{0,1:T(8,128)(2,1)}) async-done(((bf16[576,4,216]{0,2,1:T(8,128)(2,1)}, bf16[288,576]{1,0:T(8,128)(2,1)}, bf16[576,1152]{1,0:T(8,128)(2,1)}, bf16[1152,576]{0,1:T(8,128)(2,1)}), (bf16[576,4,216]{0,2,1:T(8,128)(2,1)}, bf16[288,576]{1,0:T(8,128)(2,1)}, ...) | async-done | bytes 3981328 | tf_op jit(solution)/shard_map/psum | solution.py:348
  598.0 2.0 convert_element_type.167
  600.0 2.8 reshape.375
  (300 shorter events, 91.7 us)
Async XLA Ops:
  7.2 8.7 %copy-start.51 = (bf16[3,1152]{1,0:T(4,128)(2,1)S(1)}, bf16[3,1152]{1,0:T(4,128)(2,1)}, u32[]{:S(2)}) copy-start(bf16[3,1152]{1,0:T(4,128)(2,1)} %param.18) | copy-start | bytes 20740
  7.2 7.5 %copy-start = (bf16[3,256,1152]{2,1,0:T(8,128)(2,1)S(1)}, bf16[3,256,1152]{2,1,0:T(8,128)(2,1)}, u32[]{:S(2)}) copy-start(bf16[3,256,1152]{2,1,0:T(8,128)(2,1)} %param.17) | copy-start | bytes 5308420
  7.2 8.1 %copy-start.67 = (f32[4,144]{1,0:T(4,128)S(1)}, f32[4,144]{1,0:T(4,128)}, u32[]{:S(2)}) copy-start(f32[4,144]{1,0:T(4,128)} %param.22) | copy-start | bytes 6916
  8.1 7.8 %collective-permute-start = (bf16[3,1152]{1,0:T(4,128)(2,1)S(1)}, bf16[3,1152]{1,0:T(4,128)(2,1)S(1)}, u32[]{:S(2)}, u32[]{:S(2)}) collective-permute-start(bf16[3,1152]{1,0:T(4,128)(2,1)S(1)} %fusion.68), channel_id=1, source_target_pairs={{0,16},{16,0},{1,17},{17,1},{2,18},{18,2},{3,19},{19,3},{4,20},{20... | collective-permute-start | bytes 20744 | tf_op jit(solution)/shard_map/ppermute | solution.py:112
  12.8 30.6 %collective-permute-start.2 = (bf16[576,864]{1,0:T(8,128)(2,1)S(1)}, bf16[576,864]{1,0:T(8,128)(2,1)}, u32[]{:S(2)}, u32[]{:S(2)}) collective-permute-start(bf16[576,864]{1,0:T(8,128)(2,1)S(1)} %copy.135), channel_id=1, source_target_pairs={{0,16},{16,0},{1,17},{17,1},{2,18},{18,2},{3,19},{19,3},{4,20},{20... | collective-permute-start | bytes 2985992 | tf_op jit(solution)/shard_map/ppermute | solution.py:112
  14.7 26.2 %copy-start.44 = (f32[3,256]{1,0:T(4,128)}, f32[3,256]{1,0:T(4,128)S(1)}, u32[]{:S(2)}) copy-start(f32[3,256]{1,0:T(4,128)S(1)} %broadcast_multiply_fusion.1) | copy-start | bytes 9220
  15.3 25.6 %copy-start.57 = (f32[3,256]{1,0:T(4,128)}, f32[3,256]{1,0:T(4,128)S(1)}, u32[]{:S(2)}) copy-start(f32[3,256]{1,0:T(4,128)S(1)} %fusion.72) | copy-start | bytes 9220
  16.5 22.9 %copy-start.63 = (f32[6912]{0:T(1024)S(1)}, f32[6912]{0:T(1024)}, u32[]{:S(2)}) copy-start(f32[6912]{0:T(1024)} %param.20) | copy-start | bytes 82948
  21.0 18.4 %collective-permute-start.1 = (f32[3,6912]{1,0:T(4,128)S(1)}, f32[3,6912]{1,0:T(4,128)S(1)}, u32[]{:S(2)}, u32[]{:S(2)}) collective-permute-start(f32[3,6912]{1,0:T(4,128)S(1)} %slice_select_fusion), channel_id=1, source_target_pairs={{0,16},{16,0},{1,17},{17,1},{2,18},{18,2},{3,19},{19,3},{4,20},{20... | collective-permute-start | bytes 248840 | tf_op jit(solution)/shard_map/ppermute | solution.py:112
  40.3 4.5 copy-start.33
  52.7 8.6 %copy-start.11 = (bf16[3,256,1152]{2,1,0:T(8,128)(2,1)S(1)}, bf16[3,256,1152]{2,1,0:T(8,128)(2,1)}, u32[]{:S(2)}) copy-start(bf16[3,256,1152]{2,1,0:T(8,128)(2,1)} %param.29) | copy-start | bytes 5308420
  53.8 35.5 %all-to-all-start = ((bf16[3,256,4,216]{1,3,0,2:T(8,128)(2,1)}), bf16[3,256,4,216]{1,3,0,2:T(8,128)(2,1)S(1)}, u32[]{:S(2)}, u32[]{:S(2)}) async-start(bf16[3,256,4,216]{1,3,0,2:T(8,128)(2,1)} %copy.138), calls=%async_computation | async-start | bytes 2654208 | tf_op jit(solution)/shard_map/all_to_all | solution.py:213
  58.7 47.9 %collective-permute-start.3 = (bf16[288,576]{1,0:T(8,128)(2,1)}, bf16[288,576]{1,0:T(8,128)(2,1)}, u32[]{:S(2)}, u32[]{:S(2)}) collective-permute-start(bf16[288,576]{1,0:T(8,128)(2,1)} %param.23), channel_id=1, source_target_pairs={{0,16},{16,0},{1,17},{17,1},{2,18},{18,2},{3,19},{19,3},{4,20},{20... | collective-permute-start | bytes 995336 | tf_op jit(solution)/shard_map/ppermute | solution.py:112
  59.2 64.3 %collective-permute-start.4 = (bf16[576,1152]{1,0:T(8,128)(2,1)}, bf16[576,1152]{1,0:T(8,128)(2,1)}, u32[]{:S(2)}, u32[]{:S(2)}) collective-permute-start(bf16[576,1152]{1,0:T(8,128)(2,1)} %param.25), channel_id=1, source_target_pairs={{0,16},{16,0},{1,17},{17,1},{2,18},{18,2},{3,19},{19,3},{4,20},{20... | collective-permute-start | bytes 3981320 | tf_op jit(solution)/shard_map/ppermute | solution.py:112
  60.7 66.0 %collective-permute-start.5 = (bf16[1152,576]{0,1:T(8,128)(2,1)}, bf16[1152,576]{0,1:T(8,128)(2,1)}, u32[]{:S(2)}, u32[]{:S(2)}) collective-permute-start(bf16[1152,576]{0,1:T(8,128)(2,1)} %param.27), channel_id=1, source_target_pairs={{0,16},{16,0},{1,17},{17,1},{2,18},{18,2},{3,19},{19,3},{4,20},{20... | collective-permute-start | bytes 3981320 | tf_op jit(solution)/shard_map/ppermute | solution.py:112
  98.8 21.0 %copy-start.7 = (bf16[3,1024,1,216]{1,3,2,0:T(8,128)(2,1)}, bf16[3,1024,1,216]{1,3,2,0:T(8,128)(2,1)S(1)}, u32[]{:S(2)}) copy-start(bf16[3,1024,1,216]{1,3,2,0:T(8,128)(2,1)S(1)} %get-tuple-element.325) | copy-start | bytes 3981316
  98.8 6.6 %copy-start.59 = (f32[3,1,1152]{2,1,0:T(1,128)S(1)}, f32[3,1,1152]{2,1,0:T(1,128)}, u32[]{:S(2)}) copy-start(f32[3,1,1152]{2,1,0:T(1,128)} %get-tuple-element.189) | copy-start | bytes 41476
  98.8 6.6 %copy-start.60 = (f32[3,1,1152]{2,1,0:T(1,128)S(1)}, f32[3,1,1152]{2,1,0:T(1,128)}, u32[]{:S(2)}) copy-start(f32[3,1,1152]{2,1,0:T(1,128)} %get-tuple-element.190) | copy-start | bytes 41476
  101.7 15.7 %all-to-all-start.1 = ((bf16[4,2,27648]{2,1,0:T(2,128)(2,1)}), bf16[4,2,27648]{2,1,0:T(2,128)(2,1)S(1)}, u32[]{:S(2)}, u32[]{:S(2)}) async-start(bf16[4,2,27648]{2,1,0:T(2,128)(2,1)} %reshape.412), calls=%async_computation.1 | async-start | bytes 884736 | tf_op jit(solution)/shard_map/all_to_all | solution.py:215
  105.2 62.7 %all-reduce.7.cloned.1.call-start = ((), (), s32[]{:S(2)}) async-start(), calls=%async_computation.4 | async-start | bytes 3538944 | tf_op jit(solution)/shard_map/psum | solution.py:219
  107.8 15.6 %copy-start.37 = (bf16[288,576]{1,0:T(8,128)(2,1)}, bf16[288,576]{1,0:T(8,128)(2,1)S(1)}, u32[]{:S(2)}) copy-start(bf16[288,576]{1,0:T(8,128)(2,1)S(1)} %get-tuple-element.180) | copy-start | bytes 995332
  107.8 15.6 %copy-start.39 = (bf16[288,576]{1,0:T(8,128)(2,1)}, bf16[288,576]{1,0:T(8,128)(2,1)S(1)}, u32[]{:S(2)}) copy-start(bf16[288,576]{1,0:T(8,128)(2,1)S(1)} %get-tuple-element.181) | copy-start | bytes 995332
  119.8 3.8 copy-start.23
  123.5 3.3 copy-start.24
  123.5 114.8 %all-reduce.9.cloned.1.call-start = ((), (), s32[]{:S(2)}) async-start(), calls=%async_computation.5 | async-start | bytes 3538944 | tf_op jit(solution)/shard_map/psum | solution.py:255
  126.7 41.2 %copy-start.65 = (f32[1152]{0:T(1024)S(1)}, f32[1152]{0:T(1024)}, u32[]{:S(2)}) copy-start(f32[1152]{0:T(1024)} %param.24) | copy-start | bytes 13828
  176.5 5.0 copy-start.69
  176.5 5.0 copy-start.27
  176.5 5.0 copy-start.28
  188.2 3.8 copy-start.70
  192.0 5.5 copy-start.21
  192.1 5.5 copy-start.71
  196.1 124.6 %collective-permute-start.13 = (bf16[1152,576]{0,1:T(8,128)(2,1)}, bf16[1152,576]{0,1:T(8,128)(2,1)}, u32[]{:S(2)}, u32[]{:S(2)}) collective-permute-start(bf16[1152,576]{0,1:T(8,128)(2,1)} %select_convert_fusion), channel_id=1, source_target_pairs={{0,16},{16,0},{1,17},{17,1},{2,18},{18,2},{3,19},{19,3},{4,20},{20... | collective-permute-start | bytes 3981320 | tf_op jit(solution)/shard_map/ppermute | solution.py:112
  246.0 3.3 copy-start.38
  246.0 3.3 copy-start.40
  255.1 17.8 %all-to-all-start.2 = ((bf16[3,256,4,72]{1,3,0,2:T(8,128)(2,1)}), bf16[3,256,4,72]{1,3,0,2:T(8,128)(2,1)}, u32[]{:S(2)}, u32[]{:S(2)}) async-start(bf16[3,256,4,72]{1,3,0,2:T(8,128)(2,1)} %copy.144), calls=%async_computation.2 | async-start | bytes 884736 | tf_op jit(solution)/shard_map/all_to_all | solution.py:272
  301.2 35.6 %all-to-all-start.3 = ((bf16[4,3,256,1,216]{2,4,1,3,0:T(8,128)(2,1)}), bf16[4,3,256,1,216]{2,4,1,3,0:T(8,128)(2,1)}, u32[]{:S(2)}, u32[]{:S(2)}) async-start(bf16[4,3,256,1,216]{2,4,1,3,0:T(8,128)(2,1)} %pad_maximum_fusion.10), calls=%async_computation.3 | async-start | bytes 2654208 | tf_op jit(solution)/shard_map/all_to_all | solution.py:10
  305.5 118.1 %all-reduce.11.cloned.1.call-start = ((), (), s32[]{:S(2)}) async-start(), calls=%async_computation.6 | async-start | bytes 7077888 | tf_op jit(solution)/shard_map/psum | solution.py:235
  307.9 6.2 %copy-start.54 = (f32[3,1152]{1,0:T(4,128)S(1)}, f32[3,1152]{1,0:T(4,128)}, u32[]{:S(2)}) copy-start(f32[3,1152]{1,0:T(4,128)} %get-tuple-element.129) | copy-start | bytes 41476
  307.9 6.8 %copy-start.55 = (f32[3,1152]{1,0:T(4,128)S(1)}, f32[3,1152]{1,0:T(4,128)}, u32[]{:S(2)}) copy-start(f32[3,1152]{1,0:T(4,128)} %get-tuple-element.134) | copy-start | bytes 41476
  307.9 7.4 %copy-start.53 = (f32[3,1152]{1,0:T(4,128)S(1)}, f32[3,1152]{1,0:T(4,128)}, u32[]{:S(2)}) copy-start(f32[3,1152]{1,0:T(4,128)} %get-tuple-element.137) | copy-start | bytes 41476
  308.1 11.6 %collective-permute-start.11 = (bf16[288,576]{1,0:T(8,128)(2,1)S(1)}, bf16[288,576]{1,0:T(8,128)(2,1)S(1)}, u32[]{:S(2)}, u32[]{:S(2)}) collective-permute-start(bf16[288,576]{1,0:T(8,128)(2,1)S(1)} %select_convert_fusion.3), channel_id=1, source_target_pairs={{0,16},{16,0},{1,17},{17,1},{2,18},{18,2},{3,19},{19,3},{4,20},{20... | collective-permute-start | bytes 995336 | tf_op jit(solution)/shard_map/ppermute | solution.py:112
  313.5 36.7 %collective-permute-start.12 = (bf16[576,1152]{1,0:T(8,128)(2,1)}, bf16[576,1152]{1,0:T(8,128)(2,1)}, u32[]{:S(2)}, u32[]{:S(2)}) collective-permute-start(bf16[576,1152]{1,0:T(8,128)(2,1)} %select_convert_fusion.1), channel_id=1, source_target_pairs={{0,16},{16,0},{1,17},{17,1},{2,18},{18,2},{3,19},{19,3},{4,20},{20... | collective-permute-start | bytes 3981320 | tf_op jit(solution)/shard_map/ppermute | solution.py:112
  350.1 247.9 %all-reduce.13.cloned.1.call-start = ((), (), s32[]{:S(2)}) async-start(), calls=%async_computation.7 | async-start | bytes 8257536 | tf_op jit(solution)/shard_map/psum | solution.py:348
  357.0 66.6 %copy-start.45 = (f32[3,256]{1,0:T(4,128)S(1)}, f32[3,256]{1,0:T(4,128)}, u32[]{:S(2)}) copy-start(f32[3,256]{1,0:T(4,128)} %copy-done.44) | copy-start | bytes 9220
  362.9 63.7 %copy-start.62 = (f32[3,256]{1,0:T(4,128)S(1)}, f32[3,256]{1,0:T(4,128)}, u32[]{:S(2)}) copy-start(f32[3,256]{1,0:T(4,128)} %copy-done.61) | copy-start | bytes 9220
  362.9 63.7 %copy-start.58 = (f32[3,256]{1,0:T(4,128)S(1)}, f32[3,256]{1,0:T(4,128)}, u32[]{:S(2)}) copy-start(f32[3,256]{1,0:T(4,128)} %copy-done.57) | copy-start | bytes 9220
  364.1 73.5 %collective-permute-start.10 = (bf16[576,864]{1,0:T(8,128)(2,1)}, bf16[576,864]{1,0:T(8,128)(2,1)}, u32[]{:S(2)}, u32[]{:S(2)}) collective-permute-start(bf16[576,864]{1,0:T(8,128)(2,1)} %select_convert_fusion.2), channel_id=1, source_target_pairs={{0,16},{16,0},{1,17},{17,1},{2,18},{18,2},{3,19},{19,3},{4,20},{20... | collective-permute-start | bytes 2985992 | tf_op jit(solution)/shard_map/ppermute | solution.py:112
  423.6 3.1 copy-start.34
  423.6 7.0 %copy-start.22 = (bf16[768,1152]{1,0:T(8,128)(2,1)S(1)}, bf16[768,1152]{1,0:T(8,128)(2,1)}, u32[]{:S(2)}) copy-start(bf16[768,1152]{1,0:T(8,128)(2,1)} %get-tuple-element.157) | copy-start | bytes 5308420
  423.6 7.0 %copy-start.66 = (f32[1152]{0:T(1024)S(1)}, f32[1152]{0:T(1024)}, u32[]{:S(2)}) copy-start(f32[1152]{0:T(1024)} %param.28) | copy-start | bytes 13828
  430.9 3.7 copy-start.64
  436.1 7.7 %collective-permute-start.6 = (f32[24768]{0:T(1024)}, f32[24768]{0:T(1024)}, u32[]{:S(2)}, u32[]{:S(2)}) collective-permute-start(f32[24768]{0:T(1024)} %concatenate.57), channel_id=1, source_target_pairs={{0,4},{4,0},{8,12},{12,8},{1,5},{5,1},{9,13},{13,9},{2,6},{6,2},{1... | collective-permute-start | bytes 297224 | tf_op jit(solution)/shard_map/ppermute | solution.py:112
  441.3 16.4 %copy-start.3 = (bf16[3,256,1152]{2,1,0:T(8,128)(2,1)S(1)}, bf16[3,256,1152]{2,1,0:T(8,128)(2,1)}, u32[]{:S(2)}) copy-start(bf16[3,256,1152]{2,1,0:T(8,128)(2,1)} %param.17) | copy-start | bytes 5308420
  441.3 16.4 %copy-start.9 = (bf16[3,256,1152]{2,1,0:T(8,128)(2,1)S(1)}, bf16[3,256,1152]{2,1,0:T(8,128)(2,1)}, u32[]{:S(2)}) copy-start(bf16[3,256,1152]{2,1,0:T(8,128)(2,1)} %get-tuple-element.158) | copy-start | bytes 5308420
  444.8 11.3 %collective-permute-start.7 = (f32[24768]{0:T(1024)S(1)}, f32[24768]{0:T(1024)S(1)}, u32[]{:S(2)}, u32[]{:S(2)}) collective-permute-start(f32[24768]{0:T(1024)S(1)} %add.234), channel_id=1, source_target_pairs={{0,8},{4,12},{8,0},{12,4},{1,9},{5,13},{9,1},{13,5},{2,10},{6,14},... | collective-permute-start | bytes 297224 | tf_op jit(solution)/shard_map/ppermute | solution.py:112
  456.1 5.6 copy-start.36
  456.2 5.6 collective-permute-start.8
  464.4 6.9 %copy-start.48 = (bf16[3,1152]{1,0:T(4,128)(2,1)S(1)}, bf16[3,1152]{1,0:T(4,128)(2,1)}, u32[]{:S(2)}) copy-start(bf16[3,1152]{1,0:T(4,128)(2,1)} %copy-done.47) | copy-start | bytes 20740
  464.4 6.9 %copy-start.50 = (bf16[3,1152]{1,0:T(4,128)(2,1)S(1)}, bf16[3,1152]{1,0:T(4,128)(2,1)}, u32[]{:S(2)}) copy-start(bf16[3,1152]{1,0:T(4,128)(2,1)} %copy-done.49) | copy-start | bytes 20740
  469.9 10.3 %collective-permute-start.9 = (f32[3,576]{1,0:T(4,128)S(1)}, f32[3,576]{1,0:T(4,128)S(1)}, u32[]{:S(2)}, u32[]{:S(2)}) collective-permute-start(f32[3,576]{1,0:T(4,128)S(1)} %slice_select_fusion.3), channel_id=1, source_target_pairs={{0,16},{16,0},{1,17},{17,1},{2,18},{18,2},{3,19},{19,3},{4,20},{20... | collective-permute-start | bytes 20744 | tf_op jit(solution)/shard_map/ppermute | solution.py:112
  471.2 8.9 %copy-start.52 = (bf16[3,1152]{1,0:T(4,128)(2,1)S(1)}, bf16[3,1152]{1,0:T(4,128)(2,1)}, u32[]{:S(2)}) copy-start(bf16[3,1152]{1,0:T(4,128)(2,1)} %param.18) | copy-start | bytes 20740
  598.0 4.9 copy-start.26
  600.0 4.5 copy-start.25
  (32 other events, 57.4 us)
Sparse Core Ops, SparseCore 0:
  123.6 44.2 all-reduce.6
  192.2 46.0 all-reduce.8
  350.2 73.3 all-reduce.10
  443.9 154.0 all-reduce.12
